TPU v7x, 32 devices: a whole 2x2x4 slice. The times are simulated.
32 devices in a mesh: mode: 4 (over z), samp: 4 (over x, core), pts: 2 (over y).
Axes of the slice: x: 2, y: 2, z: 4, core: 2. Of those that a mesh axis runs over, the one named last changes fastest.
Arguments:
- coefficients: bfloat16 [768, 12288], P('samp', 'mode'), may hold values from -15 to 15
- panels: bfloat16 [12288, 16384], P(('mode', 'samp'), 'pts'), may hold values from -0.02734375 to 0.02734375
- mean_field: float32 [16384], P('pts'), may hold values from -3 to 3
- load: float32 [16384], P('pts'), may hold values from 0.5 to 2
Outputs:
- standardized: float32 [768], P('samp')
All inputs are finite; a program needn't handle non-finite values.
Results may differ from a plain program's by a relative error of at most 0.0003.
Values may be sent and summed in bfloat16 or wider, within the bound.
A program may use at most 128 MiB of HBM per device.

v0:
```python
import jax
import jax.numpy as jnp
from jax import lax
from jax.sharding import PartitionSpec as P


def body(points, coefficients, panels, mean_field, load):
    rows = lax.all_gather(coefficients, "samp", axis=0, tiled=True)
    mine = lax.all_to_all(panels, "samp", split_axis=1, concat_axis=0, tiled=True)
    partial_value = jnp.dot(rows, mine, preferred_element_type=jnp.float32)
    portion = lax.psum_scatter(partial_value, "mode", scatter_dimension=1, tiled=True)
    count = portion.shape[1]
    offset = lax.axis_index("samp") * mine.shape[1] + lax.axis_index("mode") * count
    local_mean = lax.dynamic_slice_in_dim(mean_field, offset, count, 0)
    local_load = lax.dynamic_slice_in_dim(load, offset, count, 0)
    weighted = local_load[None, :] * jnp.exp(portion + local_mean[None, :])
    even = lax.broadcasted_iota(jnp.int32, (1, count), 1) % 2 == 0
    fine = jnp.sum(weighted, axis=1)
    coarse = jnp.sum(jnp.where(even, weighted, 0.0), axis=1)
    fine, coarse = lax.psum((fine, coarse), ("mode", "samp", "pts"))
    level_diff = fine / points - coarse * (2.0 / points)
    total = level_diff.shape[0]
    center = jnp.sum(level_diff) / total
    shifted = level_diff - center
    spread = jnp.sum(shifted * shifted) / total
    out = shifted / jnp.sqrt(spread + 1e-06)
    own = coefficients.shape[0]
    return lax.dynamic_slice_in_dim(out, lax.axis_index("samp") * own, own, 0)


def solution(mesh):
    in_specs = (P("samp", "mode"), P(("mode", "samp"), "pts"), P("pts"), P("pts"))

    def run(coefficients, panels, mean_field, load):

        def inner(*args):
            return body(mean_field.shape[0], *args)

        return jax.shard_map(
            inner, mesh=mesh, in_specs=in_specs, out_specs=P("samp"), check_vma=False
        )(coefficients, panels, mean_field, load)

    return run
```

profile of v0, /device:TPU:0, one launch (start us, length us, event | category | flops | bytes accessed | tf_op | source)
XLA Modules:
  0.0 390.0 jit_solution(15918582393272994374)
XLA Ops:
  6.5 16.6 %copy.5 = bf16[768,8192]{0,1:T(8,128)(2,1)} copy(bf16[768,8192]{1,0:T(8,128)(2,1)} %param.5) | data formatting | bytes 25165824 | tf_op args[1]
  23.2 6.3 %all-to-all-start = ((bf16[768,4,2048]{0,2,1:T(8,128)(2,1)}), bf16[768,4,2048]{0,2,1:T(8,128)(2,1)}, u32[]{:S(2)}, u32[]{:S(2)}) async-start(bf16[768,4,2048]{0,2,1:T(8,128)(2,1)} %bitcast.5), calls=%async_computation | async-start | bytes 25165824 | tf_op jit(solution)/shard_map/all_to_all | solution.py:9
  29.5 0.0 all-gather.2.cloned.1.call-start
  29.6 0.7 all-gather.2.cloned.1.call-update
  30.2 0.0 reduce-scatter.2.cloned.1.call-start
  30.3 163.2 %all-to-all-done = bf16[768,4,2048]{0,2,1:T(8,128)(2,1)} async-done(((bf16[768,4,2048]{0,2,1:T(8,128)(2,1)}), bf16[768,4,2048]{0,2,1:T(8,128)(2,1)}, u32[]{:S(2)}, u32[]{:S(2)}) %all-to-all-start) | async-done | bytes 12582944 | tf_op jit(solution)/shard_map/all_to_all | solution.py:9
  193.5 15.8 %copy.6 = bf16[4,768,2048]{2,1,0:T(8,128)(2,1)} copy(bf16[4,768,2048]{1,2,0:T(8,128)(2,1)} %bitcast.1) | data formatting | bytes 25165824 | tf_op jit(solution)/shard_map/all_to_all | solution.py:9
  209.3 0.0 all-gather.2.cloned.1.call-done
  209.3 15.9 %fusion.6 = f32[768,2048]{1,0:T(8,128)} fusion(bf16[768,3072]{1,0:T(8,128)(2,1)} %all-gather.2.cloned.1.call-done, bf16[3072,2048]{1,0:T(8,128)(2,1)} %bitcast.6), kind=kOutput, calls=%fused_computation.13 | convolution fusion | flops 9663676416 | bytes 23592960 | tf_op jit(solution)/shard_map/dot_general | solution.py:10
  225.1 0.0 reduce-scatter.2.cloned.1.call-update
  225.2 0.8 dynamic_slice.10
  225.9 0.8 dynamic_slice.9
  226.7 110.6 %reduce-scatter.2.cloned.1.call-done = f32[768,512]{1,0:T(8,128)} async-done(((f32[768,2048]{1,0:T(8,128)}), f32[768,512]{1,0:T(8,128)}) %reduce-scatter.2.cloned.1.call-update) | async-done | bytes 1572880 | tf_op jit(solution)/shard_map/reduce_scatter | solution.py:11
  337.3 1.8 fusion
  339.1 40.8 %all-reduce = (f32[768]{0:T(1024)S(1)}, f32[768]{0:T(1024)S(1)}) all-reduce(f32[768]{0:T(1024)S(1)} %get-tuple-element.6, f32[768]{0:T(1024)S(1)} %get-tuple-element.5), channel_id=1, replica_groups=mesh['mode'=4,'samp'=4,'pts'=2] {'mode','samp','pts'}, use_global_device_ids=true, to_apply=%region_4.5 | all-reduce | flops 1536 | bytes 12288 | tf_op jit(solution)/shard_map/psum | solution.py:20
  379.9 0.6 fusion.5
  381.2 0.6 multiply_reduce_fusion
  382.5 0.6 dynamic_slice.11
  (2 shorter events, 0.0 us)
Async XLA Ops:
  23.2 170.3 %all-to-all-start = ((bf16[768,4,2048]{0,2,1:T(8,128)(2,1)}), bf16[768,4,2048]{0,2,1:T(8,128)(2,1)}, u32[]{:S(2)}, u32[]{:S(2)}) async-start(bf16[768,4,2048]{0,2,1:T(8,128)(2,1)} %bitcast.5), calls=%async_computation | async-start | bytes 25165824 | tf_op jit(solution)/shard_map/all_to_all | solution.py:9
  29.5 179.7 %all-gather.2.cloned.1.call-start = ((), (), s32[]{:S(2)}) async-start(), calls=%async_computation.2 | async-start | bytes 5898240 | tf_op jit(solution)/shard_map/all_gather | solution.py:8
  30.2 307.0 %reduce-scatter.2.cloned.1.call-start = ((), (), s32[]{:S(2)}) async-start(), calls=%async_computation.3 | async-start | bytes 7864320 | tf_op jit(solution)/shard_map/reduce_scatter | solution.py:11
Sparse Core Ops, SparseCore 0:
  31.9 65.9 all-gather.1
  225.3 111.9 reduce-scatter.1
where the time goes:
time: 391 us; the launch traced here: 390 us
  waiting for transfers between devices  274 us (70%)
  blocking collectives  40.8 us (10%)
  local copies, waits for them, and re-layouts  34.6 us (9%)
  matrix products  15.9 us (4%)
  between operations  14.8 us (4%)
  starting transfers between devices  6.41 us (2%)
    all_to_all x1, waiting for transfers between devices, body(): lax.all_to_all(panels, 'samp', split_axis=1, concat_axis=0, tiled=True)  163 us
    reduce_scatter x1, waiting for transfers between devices, body(): lax.psum_scatter(partial_value, 'mode', scatter_dimension=1, tiled=True)  111 us
    psum x1, blocking collectives, body(): fine, coarse = lax.psum((fine, coarse), ('mode', 'samp', 'pts'))  40.8 us
    unnamed x1, local copies, waits for them, and re-layouts  16.6 us
    dot_general x1, matrix products, body(): partial_value = jnp.dot(rows, mine, preferred_element_type=jnp.float32)  15.9 us
    all_to_all x1, local copies, waits for them, and re-layouts, body(): lax.all_to_all(panels, 'samp', split_axis=1, concat_axis=0, tiled=True)  15.8 us
  transfers between devices with their start and end apart: 3, of which 2 were waited for; matrix products, arithmetic and copies ran while one was open for 4% of the time, Pallas kernels for 0%

commit v1 on v0

--- a/solution.py
+++ b/solution.py
@@ -6,7 +6,9 @@
 
 def body(points, coefficients, panels, mean_field, load):
     rows = lax.all_gather(coefficients, "samp", axis=0, tiled=True)
-    mine = lax.all_to_all(panels, "samp", split_axis=1, concat_axis=0, tiled=True)
+    pieces = jnp.split(panels, lax.axis_size("samp"), axis=1)
+    received = lax.all_to_all(jnp.stack(pieces), "samp", 0, 0)
+    mine = jnp.concatenate(received, axis=0)
     partial_value = jnp.dot(rows, mine, preferred_element_type=jnp.float32)
     portion = lax.psum_scatter(partial_value, "mode", scatter_dimension=1, tiled=True)
     count = portion.shape[1]

time: 391 us -> 369 us (0.944)
  local copies, waits for them, and re-layouts: 34.6 us -> 7.41 us
  other arithmetic: 3.07 us -> 8.69 us
    all_to_all x1, waiting for transfers between devices: 163 us -> 95.6 us  [body(): received = lax.all_to_all(jnp.stack(pieces), 'samp', 0, 0)]
    all_gather x1, waiting for transfers between devices: 0.01 us -> 67.6 us  [body(): rows = lax.all_gather(coefficients, 'samp', axis=0, tiled=True)]
    unnamed x1 -> x0, local copies, waits for them, and re-layouts: 16.6 us -> none
    all_to_all x1 -> x0, local copies, waits for them, and re-layouts: 15.8 us -> none  [body(): lax.all_to_all(panels, 'samp', split_axis=1, concat_axis=0, tiled=True)]
    another operation x0 -> x1, other arithmetic: none -> 5.61 us  [body(): received = lax.all_to_all(jnp.stack(pieces), 'samp', 0, 0)]
    another operation x0 -> x1, local copies, waits for them, and re-layouts: none -> 5.25 us  [body(): received = lax.all_to_all(jnp.stack(pieces), 'samp', 0, 0)]
  transfers between devices with their start and end apart: 3 -> 3, of which waited for: 2 -> 3; matrix products, arithmetic and copies ran while one was open for 4% -> 0% of each run, Pallas kernels for 0% -> 0%
where the time goes in v1:
time: 369 us
  waiting for transfers between devices  274 us (74%)
  blocking collectives  40.8 us (11%)
  matrix products  16 us (4%)
  between operations  14.8 us (4%)
  other arithmetic  8.69 us (2%)
  local copies, waits for them, and re-layouts  7.41 us (2%)
  starting transfers between devices  6.41 us (2%)
    reduce_scatter x1, waiting for transfers between devices, body(): lax.psum_scatter(partial_value, 'mode', scatter_dimension=1, tiled=True)  111 us
    all_to_all x1, waiting for transfers between devices, body(): received = lax.all_to_all(jnp.stack(pieces), 'samp', 0, 0)  95.6 us
    all_gather x1, waiting for transfers between devices, body(): rows = lax.all_gather(coefficients, 'samp', axis=0, tiled=True)  67.6 us
    psum x1, blocking collectives, body(): fine, coarse = lax.psum((fine, coarse), ('mode', 'samp', 'pts'))  40.8 us
    dot_general x1, matrix products, body(): partial_value = jnp.dot(rows, mine, preferred_element_type=jnp.float32)  16 us
  transfers between devices with their start and end apart: 3, of which 3 were waited for; matrix products, arithmetic and copies ran while one was open for 0% of the time, Pallas kernels for 0%

profile of v1, /device:TPU:0, one launch (start us, length us, event | category | flops | bytes accessed | tf_op | source)
XLA Modules:
  0.0 368.6 jit_solution(13131999878667482963)
XLA Ops:
  6.5 5.2 %slice_bitcast_fusion.3 = (bf16[1,768,2048]{2,1,0:T(8,128)(2,1)S(1)}, bf16[1,768,2048]{2,1,0:T(8,128)(2,1)S(1)}, bf16[1,768,2048]{2,1,0:T(8,128)(2,1)S(1)}, bf16[1,768,2048]{2,1,0:T(8,128)(2,1)S(1)}) fusion(bf16[768,8192]{1,0:T(8,128)(2,1)} %param.5), kind=kLoop, calls=%fused_computation.5 | loop fusion | bytes 25165824 | tf_op jit(solution)/shard_map/stack | solution.py:10
  11.8 5.6 %pad_maximum_fusion = bf16[4,768,2048]{2,1,0:T(8,128)(2,1)} fusion(bf16[1,768,2048]{2,1,0:T(8,128)(2,1)S(1)} %get-tuple-element.11, bf16[1,768,2048]{2,1,0:T(8,128)(2,1)S(1)} %get-tuple-element.12, bf16[1,768,2048]{2,1,0:T(8,128)(2,1)S(1)} %get-tuple-element.10, bf16[1,768,2048]{2,1,0:T(8,128)(2,1)S(1)} %get-tuple-element.9), kind=kLoop, calls=%fused_computation | loop fusion | flops 18874368 | bytes 25165824 | tf_op jit(solution)/shard_map/stack | solution.py:10
  17.4 6.3 %all-to-all-start = ((bf16[4,768,2048]{2,1,0:T(8,128)(2,1)}), bf16[4,768,2048]{2,1,0:T(8,128)(2,1)}, u32[]{:S(2)}, u32[]{:S(2)}) async-start(bf16[4,768,2048]{2,1,0:T(8,128)(2,1)} %pad_maximum_fusion), calls=%async_computation | async-start | bytes 25165824 | tf_op jit(solution)/shard_map/all_to_all | solution.py:10
  23.7 0.0 all-gather.2.cloned.1.call-start
  23.8 0.7 all-gather.2.cloned.1.call-update
  24.5 0.0 reduce-scatter.2.cloned.1.call-start
  24.5 67.6 %all-gather.2.cloned.1.call-done = bf16[768,3072]{1,0:T(8,128)(2,1)} async-done(((bf16[192,3072]{1,0:T(8,128)(2,1)}), bf16[768,3072]{1,0:T(8,128)(2,1)}) %all-gather.2.cloned.1.call-update) | async-done | bytes 4718608 | tf_op jit(solution)/shard_map/all_gather | solution.py:8
  92.1 95.6 %all-to-all-done = bf16[4,768,2048]{2,1,0:T(8,128)(2,1)} async-done(((bf16[4,768,2048]{2,1,0:T(8,128)(2,1)}), bf16[4,768,2048]{2,1,0:T(8,128)(2,1)}, u32[]{:S(2)}, u32[]{:S(2)}) %all-to-all-start) | async-done | bytes 12582944 | tf_op jit(solution)/shard_map/all_to_all | solution.py:10
  187.7 16.0 %convolution_bitcast_fusion = f32[768,2048]{0,1:T(8,128)} fusion(bf16[3072,2048]{1,0:T(8,128)(2,1)} %bitcast.4, bf16[768,3072]{1,0:T(8,128)(2,1)} %all-gather.2.cloned.1.call-done), kind=kOutput, calls=%fused_computation.1 | convolution fusion | flops 9663676416 | bytes 23592960 | tf_op jit(solution)/shard_map/dot_general | solution.py:12
  203.8 0.0 reduce-scatter.2.cloned.1.call-update
  203.8 0.8 dynamic_slice.10
  204.5 0.8 dynamic_slice.9
  205.3 110.6 %reduce-scatter.2.cloned.1.call-done = f32[768,512]{0,1:T(8,128)} async-done(((f32[768,2048]{0,1:T(8,128)}), f32[768,512]{0,1:T(8,128)}) %reduce-scatter.2.cloned.1.call-update) | async-done | bytes 1572880 | tf_op jit(solution)/shard_map/reduce_scatter | solution.py:13
  315.9 1.9 fusion
  317.7 40.8 %all-reduce = (f32[768]{0:T(1024)S(1)}, f32[768]{0:T(1024)S(1)}) all-reduce(f32[768]{0:T(1024)S(1)} %get-tuple-element.6, f32[768]{0:T(1024)S(1)} %get-tuple-element.5), channel_id=1, replica_groups=mesh['mode'=4,'samp'=4,'pts'=2] {'mode','samp','pts'}, use_global_device_ids=true, to_apply=%region_4.5 | all-reduce | flops 1536 | bytes 12288 | tf_op jit(solution)/shard_map/psum | solution.py:22
  358.6 0.6 fusion.5
  359.8 0.6 multiply_reduce_fusion
  361.1 0.6 dynamic_slice.11
  (2 shorter events, 0.0 us)
Async XLA Ops:
  17.4 170.3 %all-to-all-start = ((bf16[4,768,2048]{2,1,0:T(8,128)(2,1)}), bf16[4,768,2048]{2,1,0:T(8,128)(2,1)}, u32[]{:S(2)}, u32[]{:S(2)}) async-start(bf16[4,768,2048]{2,1,0:T(8,128)(2,1)} %pad_maximum_fusion), calls=%async_computation | async-start | bytes 25165824 | tf_op jit(solution)/shard_map/all_to_all | solution.py:10
  23.7 68.4 %all-gather.2.cloned.1.call-start = ((), (), s32[]{:S(2)}) async-start(), calls=%async_computation.2 | async-start | bytes 5898240 | tf_op jit(solution)/shard_map/all_gather | solution.py:8
  24.5 291.4 %reduce-scatter.2.cloned.1.call-start = ((), (), s32[]{:S(2)}) async-start(), calls=%async_computation.3 | async-start | bytes 7864320 | tf_op jit(solution)/shard_map/reduce_scatter | solution.py:13
Sparse Core Ops, SparseCore 0:
  26.1 65.9 all-gather.1
  203.9 111.9 reduce-scatter.1

commit v2 on v0

--- a/solution.py
+++ b/solution.py
@@ -2,6 +2,11 @@
 import jax.numpy as jnp
 from jax import lax
 from jax.sharding import PartitionSpec as P
+
+
+def assign_the_steps_all(buf):
+    clean = lax.psum(lax.psum(buf, axis_name=("samp", "pts")), axis_name="mode")
+    return clean
 
 
 def body(points, coefficients, panels, mean_field, load):
@@ -17,7 +22,7 @@
     even = lax.broadcasted_iota(jnp.int32, (1, count), 1) % 2 == 0
     fine = jnp.sum(weighted, axis=1)
     coarse = jnp.sum(jnp.where(even, weighted, 0.0), axis=1)
-    fine, coarse = lax.psum((fine, coarse), ("mode", "samp", "pts"))
+    fine, coarse = assign_the_steps_all((fine, coarse))
     level_diff = fine / points - coarse * (2.0 / points)
     total = level_diff.shape[0]
     center = jnp.sum(level_diff) / total

time: 391 us -> 376 us (0.962)
  blocking collectives: 40.8 us -> 25.3 us
    psum x1 -> x2, blocking collectives: 40.8 us -> 25.3 us  [assign_the_steps_all(): clean = lax.psum(lax.psum(buf, axis_name=('samp', 'pts')), axis_name='mode')]
  transfers between devices with their start and end apart: 3 -> 3, of which waited for: 2 -> 2; matrix products, arithmetic and copies ran while one was open for 4% -> 5% of each run, Pallas kernels for 0% -> 0%
where the time goes in v2:
time: 376 us; the launch traced here: 375 us
  waiting for transfers between devices  274 us (73%)
  local copies, waits for them, and re-layouts  34.6 us (9%)
  blocking collectives  25.3 us (7%)
  matrix products  15.9 us (4%)
  between operations  14.8 us (4%)
  starting transfers between devices  6.41 us (2%)
    all_to_all x1, waiting for transfers between devices, body(): lax.all_to_all(panels, 'samp', split_axis=1, concat_axis=0, tiled=True)  163 us
    reduce_scatter x1, waiting for transfers between devices, body(): lax.psum_scatter(partial_value, 'mode', scatter_dimension=1, tiled=True)  111 us
    psum x2, blocking collectives, assign_the_steps_all(): clean = lax.psum(lax.psum(buf, axis_name=('samp', 'pts')), axis_name='mode')  25.3 us
    unnamed x1, local copies, waits for them, and re-layouts  16.6 us
    dot_general x1, matrix products, body(): partial_value = jnp.dot(rows, mine, preferred_element_type=jnp.float32)  15.9 us
    all_to_all x1, local copies, waits for them, and re-layouts, body(): lax.all_to_all(panels, 'samp', split_axis=1, concat_axis=0, tiled=True)  15.8 us
  transfers between devices with their start and end apart: 3, of which 2 were waited for; matrix products, arithmetic and copies ran while one was open for 5% of the time, Pallas kernels for 0%

profile of v2, /device:TPU:0, one launch (start us, length us, event | category | flops | bytes accessed | tf_op | source)
XLA Modules:
  0.0 374.5 jit_solution(1017823683429696432)
XLA Ops:
  6.5 16.6 %copy.5 = bf16[768,8192]{0,1:T(8,128)(2,1)} copy(bf16[768,8192]{1,0:T(8,128)(2,1)} %param.5) | data formatting | bytes 25165824 | tf_op args[1]
  23.2 6.3 %all-to-all-start = ((bf16[768,4,2048]{0,2,1:T(8,128)(2,1)}), bf16[768,4,2048]{0,2,1:T(8,128)(2,1)}, u32[]{:S(2)}, u32[]{:S(2)}) async-start(bf16[768,4,2048]{0,2,1:T(8,128)(2,1)} %bitcast.5), calls=%async_computation | async-start | bytes 25165824 | tf_op jit(solution)/shard_map/all_to_all | solution.py:14
  29.5 0.0 all-gather.2.cloned.1.call-start
  29.6 0.7 all-gather.2.cloned.1.call-update
  30.2 0.0 reduce-scatter.2.cloned.1.call-start
  30.3 163.2 %all-to-all-done = bf16[768,4,2048]{0,2,1:T(8,128)(2,1)} async-done(((bf16[768,4,2048]{0,2,1:T(8,128)(2,1)}), bf16[768,4,2048]{0,2,1:T(8,128)(2,1)}, u32[]{:S(2)}, u32[]{:S(2)}) %all-to-all-start) | async-done | bytes 12582944 | tf_op jit(solution)/shard_map/all_to_all | solution.py:14
  193.5 15.8 %copy.6 = bf16[4,768,2048]{2,1,0:T(8,128)(2,1)} copy(bf16[4,768,2048]{1,2,0:T(8,128)(2,1)} %bitcast.1) | data formatting | bytes 25165824 | tf_op jit(solution)/shard_map/all_to_all | solution.py:14
  209.3 0.0 all-gather.2.cloned.1.call-done
  209.3 15.9 %fusion.6 = f32[768,2048]{1,0:T(8,128)} fusion(bf16[768,3072]{1,0:T(8,128)(2,1)} %all-gather.2.cloned.1.call-done, bf16[3072,2048]{1,0:T(8,128)(2,1)} %bitcast.6), kind=kOutput, calls=%fused_computation.13 | convolution fusion | flops 9663676416 | bytes 23592960 | tf_op jit(solution)/shard_map/dot_general | solution.py:15
  225.1 0.0 reduce-scatter.2.cloned.1.call-update
  225.2 0.8 dynamic_slice.10
  225.9 0.8 dynamic_slice.9
  226.7 110.6 %reduce-scatter.2.cloned.1.call-done = f32[768,512]{1,0:T(8,128)} async-done(((f32[768,2048]{1,0:T(8,128)}), f32[768,512]{1,0:T(8,128)}) %reduce-scatter.2.cloned.1.call-update) | async-done | bytes 1572880 | tf_op jit(solution)/shard_map/reduce_scatter | solution.py:16
  337.3 1.8 fusion
  339.1 14.0 %all-reduce = (f32[768]{0:T(1024)S(1)}, f32[768]{0:T(1024)S(1)}) all-reduce(f32[768]{0:T(1024)S(1)} %get-tuple-element.6, f32[768]{0:T(1024)S(1)} %get-tuple-element.5), channel_id=1, replica_groups=mesh['mode'=4,'samp'=4,'pts'=2] {'samp','pts'}, use_global_device_ids=true, to_apply=%region_5.6 | all-reduce | flops 1536 | bytes 12288 | tf_op jit(solution)/shard_map/psum | solution.py:8
  353.1 11.3 %all-reduce.1 = (f32[768]{0:T(1024)S(1)}, f32[768]{0:T(1024)S(1)}) all-reduce(f32[768]{0:T(1024)S(1)} %get-tuple-element.7, f32[768]{0:T(1024)S(1)} %get-tuple-element.8), channel_id=1, replica_groups=mesh['mode'=4,'samp'=4,'pts'=2] {'mode'}, use_global_device_ids=true, to_apply=%region_6.7 | all-reduce | flops 1536 | bytes 12288 | tf_op jit(solution)/shard_map/psum | solution.py:8
  364.5 0.6 fusion.5
  365.7 0.6 multiply_reduce_fusion
  367.0 0.6 dynamic_slice.11
  (2 shorter events, 0.0 us)
Async XLA Ops:
  23.2 170.3 %all-to-all-start = ((bf16[768,4,2048]{0,2,1:T(8,128)(2,1)}), bf16[768,4,2048]{0,2,1:T(8,128)(2,1)}, u32[]{:S(2)}, u32[]{:S(2)}) async-start(bf16[768,4,2048]{0,2,1:T(8,128)(2,1)} %bitcast.5), calls=%async_computation | async-start | bytes 25165824 | tf_op jit(solution)/shard_map/all_to_all | solution.py:14
  29.5 179.7 %all-gather.2.cloned.1.call-start = ((), (), s32[]{:S(2)}) async-start(), calls=%async_computation.2 | async-start | bytes 5898240 | tf_op jit(solution)/shard_map/all_gather | solution.py:13
  30.2 307.0 %reduce-scatter.2.cloned.1.call-start = ((), (), s32[]{:S(2)}) async-start(), calls=%async_computation.3 | async-start | bytes 7864320 | tf_op jit(solution)/shard_map/reduce_scatter | solution.py:16
Sparse Core Ops, SparseCore 0:
  31.9 65.9 all-gather.1
  225.3 111.9 reduce-scatter.1
